TPU v7x, 512 devices: a whole 4x8x8 slice. The times are simulated.
512 devices in a mesh: grp: 64 (over z, y), row: 8 (over x, core).
Axes of the slice: x: 4, y: 8, z: 8, core: 2. Of those that a mesh axis runs over, the one named last changes fastest.
Arguments:
- latents: bfloat16 [64, 16384], P('grp'), may hold values from -6 to 6
- frames: int32 [64], replicated, may hold values from 1 to 4, as said below
- offsets: int32 [64], replicated, may hold values from 0 to 1008, as said below
- assign: int32 [64], replicated, may hold values from 0 to 63, each once
- w_in: bfloat16 [16, 27, 384], replicated, may hold values from -0.3125 to 0.3125
- w_mid: bfloat16 [384, 27, 192], P('grp'), may hold values from -0.0625 to 0.0625
- w_out: bfloat16 [192, 27, 96], P('grp'), may hold values from -0.078125 to 0.078125
- gain_in: float32 [384], replicated, may hold values from 0.25 to 1.75
- gain_mid: float32 [192], replicated, may hold values from 0.25 to 1.75
- gain_out: float32 [96], replicated, may hold values from 0.25 to 1.75
Outputs:
- decoded: bfloat16 [64, 4, 64, 6144], P('grp', None, 'row')
Inputs may be any that keep to these rules, and one draw needn't show every extreme that they name: Some request has exactly 4 frames. The blocks of different requests do not intersect, and offsets[r] + 16 <= 1024 for every request; some request starts at 1008. `assign`: every request is decoded by exactly one group.
All inputs are finite; a program needn't handle non-finite values.
Results may differ from a plain program's by a relative error of at most 0.006.
Values may be sent and summed in bfloat16 or wider, within the bound.
A program may use at most 128 MiB of HBM per device.

v0:
```python
import jax
import jax.numpy as jnp
from jax import lax
from jax.sharding import PartitionSpec as P

RL = 2
WL = 16
FMAX = 4


def extended_2(cells, sides, width):
    for axis, dim in sides:
        count = lax.axis_size(axis)
        ends = count - 1
        head = lax.slice_in_dim(cells, 0, width, axis=dim)
        tail = lax.slice_in_dim(cells, cells.shape[dim] - width, cells.shape[dim], axis=dim)
        cells = jnp.concatenate(
            [
                lax.ppermute(tail, axis, [(i, (i + 1) % count) for i in range(ends)]),
                cells,
                lax.ppermute(head, axis, [((i + 1) % count, i) for i in range(ends)]),
            ],
            axis=dim,
        )
    return cells


def rms_silu(hidden, gain):
    mean_sq = jnp.mean(hidden * hidden, axis=-1, keepdims=True)
    scaled = hidden * lax.rsqrt(mean_sq + 1e-06) * gain
    return jax.nn.silu(scaled)


def causal_conv(extended, weight):
    count_t = extended.shape[0]
    count_r = extended.shape[1] - 2
    count_c = extended.shape[2]
    width_in = extended.shape[3]
    width_out = weight.shape[2]
    padded = jnp.pad(extended, ((2, 0), (0, 0), (1, 1), (0, 0)))
    total = jnp.zeros((count_t * count_r * count_c, width_out), jnp.float32)
    for time_tap in range(3):
        for row_tap in range(3):
            for col_tap in range(3):
                window = padded[
                    time_tap : time_tap + count_t,
                    row_tap : row_tap + count_r,
                    col_tap : col_tap + count_c,
                ]
                window = window.reshape(count_t * count_r * count_c, width_in)
                tap_index = 9 * time_tap + 3 * row_tap + col_tap
                total = total + jnp.dot(
                    window, weight[:, tap_index, :], preferred_element_type=jnp.float32
                )
    return total.reshape(count_t, count_r, count_c, width_out)


def upsample(values):
    return jnp.repeat(jnp.repeat(values, 2, axis=1), 2, axis=2)


def per_device(latents, frames, offsets, assign, w_in, w_mid, w_out, gain_in, gain_mid, gain_out):
    groups = lax.axis_size("grp")
    row_count = lax.axis_size("row")
    row_index = lax.axis_index("row")
    group_index = lax.axis_index("grp")
    channels = w_in.shape[0]
    cap_vals = latents.shape[1] // groups
    cap_tokens = cap_vals // channels
    span_len = cap_tokens // FMAX
    flat = latents[0]
    slot_ids = jnp.arange(cap_vals, dtype=jnp.int32)

    def select_span(request):
        start = offsets[request] * channels
        block = lax.dynamic_slice_in_dim(flat, start, cap_vals)
        keep = slot_ids < frames[request] * span_len * channels
        return jnp.where(keep, block, jnp.zeros((), block.dtype))

    outgoing = jax.vmap(select_span)(assign)
    incoming = lax.all_to_all(outgoing, "grp", split_axis=0, concat_axis=0, tiled=True)
    table = incoming.reshape(groups * cap_tokens, channels)
    request = assign[group_index]
    count = frames[request]
    fill_len = count * span_len
    image_rows = RL * row_count
    frame_ids = jnp.arange(FMAX, dtype=jnp.int32)[:, None, None]
    row_ids = row_index * RL + jnp.arange(RL, dtype=jnp.int32)[None, :, None]
    col_ids = jnp.arange(WL, dtype=jnp.int32)[None, None, :]
    position = (frame_ids * image_rows + row_ids) * WL + col_ids
    shard = jnp.minimum(position // fill_len, groups - 1)
    within = position % fill_len
    tokens = table[shard * cap_tokens + within]
    valid = (frame_ids < count)[..., None]
    latent_in = jnp.where(valid, tokens, jnp.zeros((), tokens.dtype))
    full_mid, full_out = (
        lax.all_gather(w_mid, "grp", axis=0, tiled=True),
        lax.all_gather(w_out, "grp", axis=0, tiled=True),
    )
    latent_ext = extended_2(latent_in, (("row", 1),), 1)
    act_in = rms_silu(causal_conv(latent_ext, w_in), gain_in).astype(jnp.bfloat16)
    mid_ext = extended_2(upsample(act_in), (("row", 1),), 1)
    act_mid = rms_silu(causal_conv(mid_ext, full_mid), gain_mid).astype(jnp.bfloat16)
    out_ext = extended_2(upsample(act_mid), (("row", 1),), 1)
    final = rms_silu(causal_conv(out_ext, full_out), gain_out)
    final = jnp.where(valid, final, jnp.zeros((), jnp.float32)).astype(jnp.bfloat16)
    return final.reshape(1, FMAX, 4 * RL, 4 * WL * final.shape[3])


def solution(mesh):
    placed = (
        P("grp", None),
        P(),
        P(),
        P(),
        P(),
        P("grp", None, None),
        P("grp", None, None),
        P(),
        P(),
        P(),
    )
    return jax.shard_map(
        per_device,
        mesh=mesh,
        in_specs=placed,
        out_specs=P("grp", None, "row", None),
        check_vma=False,
    )
```

profile of v0, /device:TPU:1, one launch (start us, length us, event | category | flops | bytes accessed | tf_op | source)
XLA Modules:
  0.0 352.4 jit_solution(12229377863620362657)
XLA Ops:
  7.9 0.8 gather_fusion.1
  8.7 1.4 gather_fusion
  10.2 1.0 reduce.3
  11.2 94.7 %while.1 = (s32[]{:T(128)}, bf16[16384]{0:T(1024)(128)(2,1)S(1)}, s32[64,1]{0,1:T(1,128)S(1)}, bf16[64,256]{1,0:T(8,128)(2,1)S(1)}, s32[]{:T(128)}, /*index=5*/s32[]{:T(128)}) while((s32[]{:T(128)}, bf16[16384]{0:T(1024)(128)(2,1)S(1)}, s32[64,1]{0,1:T(1,128)S(1)}, bf16[64,256]{1,0:T(8,128)(2,1)S(1)}, s32[]{:T(128)}, /*index=5*/s32[]{:T(128)}) %tuple.141), condition=%wide.while_cond, body=%wide.while_body.sunk | while | flops 2 | bytes 3169 | solution.py:76
  77.0 0.8 dynamic-slice.7
  84.4 0.8 dynamic-slice.7
  88.8 0.8 dynamic-slice.7
  99.2 0.8 dynamic-slice.7
  107.8 17.2 %all-to-all-start = ((bf16[64,2,128]{2,1,0:T(2,128)(2,1)}), bf16[64,2,128]{2,1,0:T(2,128)(2,1)S(1)}, u32[]{:S(2)}, u32[]{:S(2)}) async-start(bf16[64,2,128]{2,1,0:T(2,128)(2,1)} %reshape.702), calls=%async_computation | async-start | bytes 65536 | tf_op jit(solution)/shard_map/all_to_all | solution.py:81
  125.1 1.3 dynamic_slice.6
  128.5 1.3 dynamic_slice.7
  131.8 4.0 %all-to-all-done = bf16[64,2,128]{2,1,0:T(2,128)(2,1)S(1)} async-done(((bf16[64,2,128]{2,1,0:T(2,128)(2,1)}), bf16[64,2,128]{2,1,0:T(2,128)(2,1)S(1)}, u32[]{:S(2)}, u32[]{:S(2)}) %all-to-all-start) | async-done | bytes 32800 | tf_op jit(solution)/shard_map/all_to_all | solution.py:81
  137.1 5.1 %collective-permute-start = (bf16[4,1,16,16]{3,2,1,0:T(8,128)(2,1)S(1)}, bf16[4,1,16,16]{3,2,1,0:T(8,128)(2,1)S(1)}, u32[]{:S(2)}, u32[]{:S(2)}) collective-permute-start(bf16[4,1,16,16]{3,2,1,0:T(8,128)(2,1)S(1)} %get-tuple-element.157), channel_id=1, source_target_pairs={{0,1},{1,2},{2,3},{3,4},{4,5},{5,6},{6,7},{8,9},{9,10},{10,11},{11... | collective-permute-start | bytes 6152 | tf_op jit(solution)/shard_map/ppermute | solution.py:19
  142.2 1.9 collective-permute-start.1
  144.2 37.3 %all_gather.7 = bf16[192,27,96]{2,1,0:T(8,128)(2,1)S(1)} all-gather(bf16[3,27,96]{2,1,0:T(8,128)(2,1)S(1)} %copy-done.91), channel_id=1, replica_groups=mesh['grp'=64,'row'=8] {'grp'}, dimensions={0}, use_global_device_ids=true | all-gather | bytes 1010880 | tf_op jit(solution)/shard_map/all_gather | solution.py:98
  186.6 14.6 %collective-permute-start.2 = (bf16[4,1,32,384]{3,2,1,0:T(8,128)(2,1)S(1)}, bf16[4,1,32,384]{3,2,1,0:T(8,128)(2,1)S(1)}, u32[]{:S(2)}, u32[]{:S(2)}) collective-permute-start(bf16[4,1,32,384]{3,2,1,0:T(8,128)(2,1)S(1)} %get-tuple-element.129), channel_id=1, source_target_pairs={{0,1},{1,2},{2,3},{3,4},{4,5},{5,6},{6,7},{8,9},{9,10},{10,11},{11... | collective-permute-start | bytes 294920 | tf_op jit(solution)/shard_map/ppermute | solution.py:19
  201.2 2.4 collective-permute-start.3
  203.6 2.8 fusion.132
  206.4 1.0 reshape.618
  207.4 1.0 pad_maximum_fusion.2
  208.7 1.4 fusion.135
  210.1 3.3 fusion.134
  213.5 8.5 %fusion.129 = (bf16[384,1,192]{2,1,0:T(2,128)(2,1)}, bf16[384,1,192]{2,1,0:T(2,128)(2,1)}, bf16[384,1,192]{2,1,0:T(2,128)(2,1)}, bf16[384,1,192]{2,1,0:T(2,128)(...) fusion(bf16[384,27,192]{2,1,0:T(8,128)(2,1)} %all-gather.2.clon, ...), kind=kLoop, calls=%fused_computation.270 | loop fusion | bytes 2359296 | tf_op jit(solution)/shard_map/slice | solution.py:53
  222.0 1.8 copy.135
  223.8 1.8 copy.134
  225.6 1.8 copy.133
  227.4 1.2 copy.132
  228.6 1.1 copy.131
  229.7 1.2 copy.130
  230.9 1.1 copy.129
  232.0 1.2 copy.155
  233.2 16.4 %fusion.128 = (bf16[384,1,192]{2,1,0:T(2,128)(2,1)}, bf16[384,1,192]{2,1,0:T(2,128)(2,1)}, bf16[384,1,192]{2,1,0:T(2,128)(2,1)}, bf16[384,1,192]{2,1,0:T(2,128)(...) fusion(bf16[384,27,192]{2,1,0:T(8,128)(2,1)} %all-gather.2.clon, ...), kind=kLoop, calls=%fused_computation.269 | loop fusion | bytes 5603328 | tf_op jit(solution)/shard_map/slice | solution.py:53
  249.6 1.8 copy.154
  251.4 1.8 copy.153
  253.2 1.8 copy.152
  255.0 1.8 copy.151
  256.8 1.8 copy.150
  258.6 1.8 copy.149
  260.4 1.8 copy.148
  262.2 1.8 copy.147
  264.0 1.8 copy.146
  265.8 1.8 copy.145
  267.6 1.1 copy.144
  268.7 1.8 copy.143
  270.5 1.1 copy.142
  271.7 1.2 copy.141
  272.9 1.8 copy.140
  274.7 1.8 copy.139
  276.5 1.8 copy.138
  278.3 1.1 copy.137
  279.4 1.3 copy.136
  280.8 1.3 fusion.64
  282.1 1.3 fusion.36
  283.4 1.2 fusion.43
  293.7 1.8 broadcast_in_dim.66
  295.5 2.1 reshape.625
  298.3 3.6 %collective-permute-start.4 = (bf16[4,1,64,192]{3,2,1,0:T(8,128)(2,1)}, bf16[4,1,64,192]{3,2,1,0:T(8,128)(2,1)S(1)}, u32[]{:S(2)}, u32[]{:S(2)}) collective-permute-start(bf16[4,1,64,192]{3,2,1,0:T(8,128)(2,1)} %get-tuple-element.125), channel_id=1, source_target_pairs={{0,1},{1,2},{2,3},{3,4},{4,5},{5,6},{6,7},{8,9},{9,10},{10,11},{11... | collective-permute-start | bytes 294920 | tf_op jit(solution)/shard_map/ppermute | solution.py:19
  301.9 1.9 collective-permute-start.5
  303.9 1.3 fusion.133
  305.2 2.9 reshape.648
  308.4 2.0 fusion.9
  310.5 3.1 fusion.131
  313.5 7.9 %fusion.130 = (bf16[4,8,64,192]{3,2,1,0:T(8,128)(2,1)S(1)}, bf16[4,8,64,192]{3,2,1,0:T(8,128)(2,1)S(1)}, bf16[4,8,64,192]{3,2,1,0:T(8,128)(2,1)S(1)}, bf16[4,8,6...) fusion(bf16[6,10,66,192]{3,2,1,0:T(8,128)(2,1)S(1)} %fusion.9), kind=kLoop, calls=%fused_computation.271 | loop fusion | bytes 29884416 | tf_op jit(solution)/shard_map/slice | solution.py:45
  344.3 1.0 select_convert_fusion
  (578 shorter events, 134.2 us)
Async XLA Ops:
  6.5 1.4 copy-start
  6.5 137.6 %copy-start.91 = (bf16[3,27,96]{2,1,0:T(8,128)(2,1)S(1)}, bf16[3,27,96]{2,1,0:T(8,128)(2,1)}, u32[]{:S(2)}) copy-start(bf16[3,27,96]{2,1,0:T(8,128)(2,1)} %param.16) | copy-start | bytes 46660
  6.5 206.9 %all-gather.2.cloned.1.call-start = ((), (), s32[]{:S(2)}) async-start(), calls=%async_computation.1 | async-start | bytes 6389760 | tf_op jit(solution)/shard_map/all_gather | solution.py:97
  107.8 73.9 %copy-start.69 = (bf16[16,27,384]{2,0,1:T(8,128)(2,1)S(1)}, bf16[16,27,384]{2,0,1:T(8,128)(2,1)}, u32[]{:S(2)}) copy-start(bf16[16,27,384]{2,0,1:T(8,128)(2,1)} %param.14) | copy-start | bytes 995332
  107.8 28.1 %all-to-all-start = ((bf16[64,2,128]{2,1,0:T(2,128)(2,1)}), bf16[64,2,128]{2,1,0:T(2,128)(2,1)S(1)}, u32[]{:S(2)}, u32[]{:S(2)}) async-start(bf16[64,2,128]{2,1,0:T(2,128)(2,1)} %reshape.702), calls=%async_computation | async-start | bytes 65536 | tf_op jit(solution)/shard_map/all_to_all | solution.py:81
  137.1 44.4 %collective-permute-start = (bf16[4,1,16,16]{3,2,1,0:T(8,128)(2,1)S(1)}, bf16[4,1,16,16]{3,2,1,0:T(8,128)(2,1)S(1)}, u32[]{:S(2)}, u32[]{:S(2)}) collective-permute-start(bf16[4,1,16,16]{3,2,1,0:T(8,128)(2,1)S(1)} %get-tuple-element.157), channel_id=1, source_target_pairs={{0,1},{1,2},{2,3},{3,4},{4,5},{5,6},{6,7},{8,9},{9,10},{10,11},{11... | collective-permute-start | bytes 6152 | tf_op jit(solution)/shard_map/ppermute | solution.py:19
  142.2 39.3 %collective-permute-start.1 = (bf16[4,1,16,16]{3,2,1,0:T(8,128)(2,1)S(1)}, bf16[4,1,16,16]{3,2,1,0:T(8,128)(2,1)S(1)}, u32[]{:S(2)}, u32[]{:S(2)}) collective-permute-start(bf16[4,1,16,16]{3,2,1,0:T(8,128)(2,1)S(1)} %get-tuple-element.158), channel_id=1, source_target_pairs={{1,0},{2,1},{3,2},{4,3},{5,4},{6,5},{7,6},{9,8},{10,9},{11,10},{12... | collective-permute-start | bytes 6152 | tf_op jit(solution)/shard_map/ppermute | solution.py:21
  184.4 1.6 copy-start.92
  186.6 20.8 %collective-permute-start.2 = (bf16[4,1,32,384]{3,2,1,0:T(8,128)(2,1)S(1)}, bf16[4,1,32,384]{3,2,1,0:T(8,128)(2,1)S(1)}, u32[]{:S(2)}, u32[]{:S(2)}) collective-permute-start(bf16[4,1,32,384]{3,2,1,0:T(8,128)(2,1)S(1)} %get-tuple-element.129), channel_id=1, source_target_pairs={{0,1},{1,2},{2,3},{3,4},{4,5},{5,6},{6,7},{8,9},{9,10},{10,11},{11... | collective-permute-start | bytes 294920 | tf_op jit(solution)/shard_map/ppermute | solution.py:19
  201.2 6.2 %collective-permute-start.3 = (bf16[4,1,32,384]{3,2,1,0:T(8,128)(2,1)S(1)}, bf16[4,1,32,384]{3,2,1,0:T(8,128)(2,1)S(1)}, u32[]{:S(2)}, u32[]{:S(2)}) collective-permute-start(bf16[4,1,32,384]{3,2,1,0:T(8,128)(2,1)S(1)} %get-tuple-element.130), channel_id=1, source_target_pairs={{1,0},{2,1},{3,2},{4,3},{5,4},{6,5},{7,6},{9,8},{10,9},{11,10},{12... | collective-permute-start | bytes 294920 | tf_op jit(solution)/shard_map/ppermute | solution.py:21
  268.7 12.1 %copy-start.22 = (bf16[4,4,32,384]{3,2,1,0:T(8,128)(2,1)S(1)}, bf16[4,4,32,384]{3,2,1,0:T(8,128)(2,1)}, u32[]{:S(2)}) copy-start(bf16[4,4,32,384]{3,2,1,0:T(8,128)(2,1)} %get-tuple-element.121) | copy-start | bytes 1179652
  271.7 10.3 %copy-start.21 = (bf16[4,4,32,384]{3,2,1,0:T(8,128)(2,1)S(1)}, bf16[4,4,32,384]{3,2,1,0:T(8,128)(2,1)}, u32[]{:S(2)}) copy-start(bf16[4,4,32,384]{3,2,1,0:T(8,128)(2,1)} %get-tuple-element.122) | copy-start | bytes 1179652
  272.9 10.5 %copy-start.23 = (bf16[4,4,32,384]{3,2,1,0:T(8,128)(2,1)S(1)}, bf16[4,4,32,384]{3,2,1,0:T(8,128)(2,1)}, u32[]{:S(2)}) copy-start(bf16[4,4,32,384]{3,2,1,0:T(8,128)(2,1)} %get-tuple-element.102) | copy-start | bytes 1179652
  279.4 5.5 %copy-start.43 = (bf16[4,4,32,384]{3,2,1,0:T(8,128)(2,1)S(1)}, bf16[4,4,32,384]{3,2,1,0:T(8,128)(2,1)}, u32[]{:S(2)}) copy-start(bf16[4,4,32,384]{3,2,1,0:T(8,128)(2,1)} %get-tuple-element.119) | copy-start | bytes 1179652
  280.7 3.8 %copy-start.44 = (bf16[4,4,32,384]{3,2,1,0:T(8,128)(2,1)S(1)}, bf16[4,4,32,384]{3,2,1,0:T(8,128)(2,1)}, u32[]{:S(2)}) copy-start(bf16[4,4,32,384]{3,2,1,0:T(8,128)(2,1)} %get-tuple-element.120) | copy-start | bytes 1179652
  280.7 3.8 %copy-start.61 = (bf16[384,1,192]{0,2,1:T(8,128)(2,1)S(1)}, bf16[384,1,192]{0,2,1:T(8,128)(2,1)}, u32[]{:S(2)}) copy-start(bf16[384,1,192]{0,2,1:T(8,128)(2,1)} %copy.130) | copy-start | bytes 442372
  280.8 4.2 %copy-start.59 = (bf16[384,1,192]{0,2,1:T(8,128)(2,1)S(1)}, bf16[384,1,192]{0,2,1:T(8,128)(2,1)}, u32[]{:S(2)}) copy-start(bf16[384,1,192]{0,2,1:T(8,128)(2,1)} %copy.131) | copy-start | bytes 442372
  282.1 3.2 copy-start.42
  282.1 3.2 copy-start.57
  285.3 1.1 copy-start.51
  285.6 1.1 copy-start.68
  285.9 1.1 copy-start.67
  286.3 1.1 copy-start.36
  286.3 1.1 copy-start.66
  286.7 1.1 copy-start.65
  287.0 1.1 copy-start.34
  287.0 1.1 copy-start.64
  287.4 1.1 copy-start.63
  287.7 1.1 copy-start.62
  288.1 1.1 copy-start.60
  288.4 1.1 copy-start.58
  288.8 1.1 copy-start.56
  289.2 1.1 copy-start.54
  289.5 1.1 copy-start.52
  289.9 1.1 copy-start.50
  290.2 1.1 copy-start.49
  290.6 1.1 copy-start.48
  290.9 1.1 copy-start.47
  291.3 1.1 copy-start.46
  291.7 1.1 copy-start.45
  295.5 9.6 %copy-start.94 = (f32[96]{0:T(128)S(1)}, f32[96]{0:T(128)}, u32[]{:S(2)}) copy-start(f32[96]{0:T(128)} %param.19) | copy-start | bytes 1156
  298.3 9.8 %collective-permute-start.4 = (bf16[4,1,64,192]{3,2,1,0:T(8,128)(2,1)}, bf16[4,1,64,192]{3,2,1,0:T(8,128)(2,1)S(1)}, u32[]{:S(2)}, u32[]{:S(2)}) collective-permute-start(bf16[4,1,64,192]{3,2,1,0:T(8,128)(2,1)} %get-tuple-element.125), channel_id=1, source_target_pairs={{0,1},{1,2},{2,3},{3,4},{4,5},{5,6},{6,7},{8,9},{9,10},{10,11},{11... | collective-permute-start | bytes 294920 | tf_op jit(solution)/shard_map/ppermute | solution.py:19
  301.9 6.5 %collective-permute-start.5 = (bf16[4,1,64,192]{3,2,1,0:T(8,128)(2,1)}, bf16[4,1,64,192]{3,2,1,0:T(8,128)(2,1)S(1)}, u32[]{:S(2)}, u32[]{:S(2)}) collective-permute-start(bf16[4,1,64,192]{3,2,1,0:T(8,128)(2,1)} %get-tuple-element.126), channel_id=1, source_target_pairs={{1,0},{2,1},{3,2},{4,3},{5,4},{6,5},{7,6},{9,8},{10,9},{11,10},{12... | collective-permute-start | bytes 294920 | tf_op jit(solution)/shard_map/ppermute | solution.py:21
  321.9 1.2 copy-start.16
  321.9 1.2 copy-start.74
  322.4 1.3 copy-start.15
  322.4 1.3 copy-start.73
  323.2 1.3 copy-start.14
  323.7 1.3 copy-start.13
  324.5 1.3 copy-start.12
  325.0 1.3 copy-start.11
  325.8 1.3 copy-start.10
  326.3 1.4 copy-start.9
  327.3 1.4 copy-start.8
  328.3 1.4 copy-start.7
  329.2 1.4 copy-start.6
  330.2 1.4 copy-start.5
  331.2 1.4 copy-start.4
  332.2 1.4 copy-start.3
  333.1 1.4 copy-start.2
  339.1 1.2 copy-start.17
  339.1 1.2 copy-start.77
  339.6 1.2 copy-start.76
  343.3 2.0 copy-start.1
  (39 other events, 40.0 us)
Sparse Core Ops, SparseCore 0:
  10.3 95.0 all-gather.1
where the time goes:
time: 359 us; the launch traced here: 352 us
  local copies, waits for them, and re-layouts  208 us (58%)
  starting transfers between devices  46.8 us (13%)
  blocking collectives  37.3 us (10%)
  matrix products  27.2 us (8%)
  between operations  18.1 us (5%)
  other arithmetic  9.07 us (3%)
  waiting for transfers between devices  5.1 us (1%)
    gather x256, local copies, waits for them, and re-layouts  94.3 us
    unnamed x219, local copies, waits for them, and re-layouts  51.6 us
    all_gather x1, blocking collectives, per_device(): lax.all_gather(w_out, 'grp', axis=0, tiled=True)  37.3 us
    slice x4, local copies, waits for them, and re-layouts, causal_conv(): weight[:, tap_index, :]  29.1 us
    dot_general x81, matrix products, causal_conv(): jnp.dot(window, weight[:, tap_index, :], preferred_element_type=jnp.float32)  27.2 us
    ppermute x3, starting transfers between devices, extended_2(): lax.ppermute(tail, axis, [(i, (i + 1) % count) for i in range(ends)])  23.3 us
    all_to_all x1, starting transfers between devices, per_device(): lax.all_to_all(outgoing, 'grp', split_axis=0, concat_axis=0, tiled=True)  17.2 us
    slice x6, local copies, waits for them, and re-layouts, causal_conv(): padded[time_tap:time_tap + count_t, row_tap:row_tap + count_r, col_tap:co...  15.8 us
  transfers between devices with their start and end apart: 8, of which 2 were waited for; matrix products, arithmetic and copies ran while one was open for 35% of the time, Pallas kernels for 0%

commit v1 on v0

--- a/solution.py
+++ b/solution.py
@@ -93,9 +93,22 @@
     tokens = table[shard * cap_tokens + within]
     valid = (frame_ids < count)[..., None]
     latent_in = jnp.where(valid, tokens, jnp.zeros((), tokens.dtype))
+
+    def measure_scenes_all(field_in):
+        newest = jnp.concatenate(
+            lax.all_to_all(
+                jnp.stack(tuple((field_in for _ in range(lax.axis_size("grp"))))),
+                split_axis=0,
+                concat_axis=0,
+                axis_name="grp",
+            ),
+            axis=0,
+        )
+        return newest
+
     full_mid, full_out = (
         lax.all_gather(w_mid, "grp", axis=0, tiled=True),
-        lax.all_gather(w_out, "grp", axis=0, tiled=True),
+        measure_scenes_all(w_out),
     )
     latent_ext = extended_2(latent_in, (("row", 1),), 1)
     act_in = rms_silu(causal_conv(latent_ext, w_in), gain_in).astype(jnp.bfloat16)

time: 359 us -> 388 us (1.081)
  waiting for transfers between devices: 5.1 us -> 84.1 us
  blocking collectives: 37.3 us -> 0 us
  local copies, waits for them, and re-layouts: 208 us -> 198 us
    all_gather x1, waiting for transfers between devices: 0.02 us -> 56.3 us  [per_device(): lax.all_gather(w_mid, 'grp', axis=0, tiled=True)]
    all_gather x1 -> x0, blocking collectives: 37.3 us -> none  [per_device(): lax.all_gather(w_out, 'grp', axis=0, tiled=True)]
    all_to_all x0 -> x1, waiting for transfers between devices: none -> 20.4 us  [measure_scenes_all(): lax.all_to_all(jnp.stack(tuple((field_in for _ in range(lax.axis_size('gr...]
    gather x256, local copies, waits for them, and re-layouts: 94.3 us -> 82.2 us
    ppermute x3, starting transfers between devices: 23.3 us -> 13.9 us  [extended_2(): lax.ppermute(tail, axis, [(i, (i + 1) % count) for i in range(ends)])]
    all_to_all x0 -> x1, starting transfers between devices: none -> 6.72 us  [measure_scenes_all(): lax.all_to_all(jnp.stack(tuple((field_in for _ in range(lax.axis_size('gr...]
    unnamed x219 -> x221, local copies, waits for them, and re-layouts: 51.6 us -> 51.4 us
  transfers between devices with their start and end apart: 8 -> 9, of which waited for: 2 -> 5; matrix products, arithmetic and copies ran while one was open for 35% -> 6% of each run, Pallas kernels for 0% -> 0%
where the time goes in v1:
time: 388 us; the launch traced here: 381 us
  local copies, waits for them, and re-layouts  198 us (51%)
  waiting for transfers between devices  84.1 us (22%)
  starting transfers between devices  44 us (11%)
  matrix products  27.2 us (7%)
  between operations  17.6 us (5%)
  other arithmetic  8.91 us (2%)
    gather x256, local copies, waits for them, and re-layouts  82.2 us
    all_gather x1, waiting for transfers between devices, per_device(): lax.all_gather(w_mid, 'grp', axis=0, tiled=True)  56.3 us
    unnamed x221, local copies, waits for them, and re-layouts  51.4 us
    slice x4, local copies, waits for them, and re-layouts, causal_conv(): weight[:, tap_index, :]  29.6 us
    dot_general x81, matrix products, causal_conv(): jnp.dot(window, weight[:, tap_index, :], preferred_element_type=jnp.float32)  27.2 us
    all_to_all x1, waiting for transfers between devices, measure_scenes_all(): lax.all_to_all(jnp.stack(tuple((field_in for _ in range(lax.axis_size('gr...  20.4 us
    all_to_all x1, starting transfers between devices, per_device(): lax.all_to_all(outgoing, 'grp', split_axis=0, concat_axis=0, tiled=True)  17.1 us
    slice x6, local copies, waits for them, and re-layouts, causal_conv(): padded[time_tap:time_tap + count_t, row_tap:row_tap + count_r, col_tap:co...  15.8 us
  transfers between devices with their start and end apart: 9, of which 5 were waited for; matrix products, arithmetic and copies ran while one was open for 6% of the time, Pallas kernels for 0%

profile of v1, /device:TPU:1, one launch (start us, length us, event | category | flops | bytes accessed | tf_op | source)
XLA Modules:
  0.0 380.7 jit_solution(7064072621599672120)
XLA Ops:
  7.2 0.8 gather_fusion.1
  8.0 1.4 gather_fusion
  9.5 1.0 reduce.3
  10.5 82.7 %while.1 = (s32[]{:T(128)}, bf16[16384]{0:T(1024)(128)(2,1)S(1)}, s32[64,1]{0,1:T(1,128)S(1)}, bf16[64,256]{1,0:T(8,128)(2,1)S(1)}, s32[]{:T(128)}, /*index=5*/s32[]{:T(128)}) while((s32[]{:T(128)}, bf16[16384]{0:T(1024)(128)(2,1)S(1)}, s32[64,1]{0,1:T(1,128)S(1)}, bf16[64,256]{1,0:T(8,128)(2,1)S(1)}, s32[]{:T(128)}, /*index=5*/s32[]{:T(128)}) %tuple.141), condition=%wide.while_cond, body=%wide.while_body.sunk | while | flops 2 | bytes 3169 | solution.py:76
  95.1 17.1 %all-to-all-start = ((bf16[64,2,128]{2,1,0:T(2,128)(2,1)}), bf16[64,2,128]{2,1,0:T(2,128)(2,1)S(1)}, u32[]{:S(2)}, u32[]{:S(2)}) async-start(bf16[64,2,128]{2,1,0:T(2,128)(2,1)} %reshape.708), calls=%async_computation | async-start | bytes 65536 | tf_op jit(solution)/shard_map/all_to_all | solution.py:81
  112.3 1.2 dynamic_slice.6
  115.2 1.2 dynamic_slice.7
  118.3 4.7 %all-to-all-done = bf16[64,2,128]{2,1,0:T(2,128)(2,1)S(1)} async-done(((bf16[64,2,128]{2,1,0:T(2,128)(2,1)}), bf16[64,2,128]{2,1,0:T(2,128)(2,1)S(1)}, u32[]{:S(2)}, u32[]{:S(2)}) %all-to-all-start) | async-done | bytes 32800 | tf_op jit(solution)/shard_map/all_to_all | solution.py:81
  124.2 5.1 %collective-permute-start = (bf16[4,1,16,16]{3,2,1,0:T(8,128)(2,1)S(1)}, bf16[4,1,16,16]{3,2,1,0:T(8,128)(2,1)S(1)}, u32[]{:S(2)}, u32[]{:S(2)}) collective-permute-start(bf16[4,1,16,16]{3,2,1,0:T(8,128)(2,1)S(1)} %get-tuple-element.157), channel_id=1, source_target_pairs={{0,1},{1,2},{2,3},{3,4},{4,5},{5,6},{6,7},{8,9},{9,10},{10,11},{11... | collective-permute-start | bytes 6152 | tf_op jit(solution)/shard_map/ppermute | solution.py:19
  129.3 1.9 collective-permute-start.1
  131.3 1.4 stack.2
  132.7 6.7 %all-to-all-start.1 = ((bf16[64,3,27,96]{3,2,1,0:T(8,128)(2,1)}), bf16[64,3,27,96]{3,2,1,0:T(8,128)(2,1)S(1)}, u32[]{:S(2)}, u32[]{:S(2)}) async-start(bf16[64,3,27,96]{3,2,1,0:T(8,128)(2,1)} %stack.2), calls=%async_computation.1 | async-start | bytes 3145728 | tf_op jit(solution)/shard_map/all_to_all | solution.py:99
  144.6 3.9 %collective-permute-start.2 = (bf16[4,1,32,384]{3,2,1,0:T(8,128)(2,1)S(1)}, bf16[4,1,32,384]{3,2,1,0:T(8,128)(2,1)S(1)}, u32[]{:S(2)}, u32[]{:S(2)}) collective-permute-start(bf16[4,1,32,384]{3,2,1,0:T(8,128)(2,1)S(1)} %get-tuple-element.129), channel_id=1, source_target_pairs={{0,1},{1,2},{2,3},{3,4},{4,5},{5,6},{6,7},{8,9},{9,10},{10,11},{11... | collective-permute-start | bytes 294920 | tf_op jit(solution)/shard_map/ppermute | solution.py:19
  148.6 2.4 collective-permute-start.3
  151.6 0.9 reshape.623
  152.6 2.3 collective-permute-done.3
  154.9 1.0 pad_maximum_fusion.2
  156.2 1.4 fusion.189
  157.6 3.3 fusion.188
  160.9 20.4 %all-to-all-done.1 = bf16[64,3,27,96]{3,2,1,0:T(8,128)(2,1)S(1)} async-done(((bf16[64,3,27,96]{3,2,1,0:T(8,128)(2,1)}), bf16[64,3,27,96]{3,2,1,0:T(8,128)(2,1)S(1)}, u32[]{:S(2)}, u32[]{:S(2)}) %all-to-all-start.1) | async-done | bytes 995360 | tf_op jit(solution)/shard_map/all_to_all | solution.py:99
  181.3 2.7 fusion.186
  184.0 56.3 %all-gather.2.cloned.1.call-done = bf16[384,27,192]{2,1,0:T(8,128)(2,1)} async-done(((bf16[6,27,192]{2,1,0:T(8,128)(2,1)}), bf16[384,27,192]{2,1,0:T(8,128)(2,1)}) %all-gather.2.cloned.1.call-update) | async-done | bytes 3981328 | tf_op jit(solution)/shard_map/all_gather | solution.py:110
  240.3 8.7 %fusion.183 = (bf16[384,1,192]{2,1,0:T(2,128)(2,1)}, bf16[384,1,192]{2,1,0:T(2,128)(2,1)}, bf16[384,1,192]{2,1,0:T(2,128)(2,1)}, bf16[384,1,192]{2,1,0:T(2,128)(...) fusion(bf16[384,27,192]{2,1,0:T(8,128)(2,1)} %all-gather.2.clon, ...), kind=kLoop, calls=%fused_computation.297 | loop fusion | bytes 2359296 | tf_op jit(solution)/shard_map/slice | solution.py:53
  249.0 1.8 copy.111
  250.8 1.8 copy.110
  252.6 1.8 copy.109
  254.4 1.1 copy.108
  255.6 1.1 copy.107
  256.7 1.2 copy.106
  257.9 1.1 copy.105
  259.0 1.2 copy.131
  260.2 16.7 %fusion.182 = (bf16[384,1,192]{2,1,0:T(2,128)(2,1)}, bf16[384,1,192]{2,1,0:T(2,128)(2,1)}, bf16[384,1,192]{2,1,0:T(2,128)(2,1)}, bf16[384,1,192]{2,1,0:T(2,128)(...) fusion(bf16[384,27,192]{2,1,0:T(8,128)(2,1)} %all-gather.2.clon, ...), kind=kLoop, calls=%fused_computation.296 | loop fusion | bytes 5603328 | tf_op jit(solution)/shard_map/slice | solution.py:53
  276.9 1.8 copy.130
  278.7 1.8 copy.129
  280.5 1.8 copy.128
  282.3 1.8 copy.127
  284.1 1.8 copy.126
  285.9 1.8 copy.125
  287.7 1.8 copy.124
  289.5 1.8 copy.123
  291.3 1.8 copy.122
  293.1 1.8 copy.121
  294.9 1.2 copy.120
  296.0 1.9 copy.119
  297.9 1.2 copy.118
  299.1 1.1 copy.117
  300.2 1.8 copy.116
  302.0 1.8 copy.115
  303.8 1.8 copy.114
  305.6 1.2 copy.113
  306.8 1.3 copy.112
  308.1 1.3 fusion.64
  309.4 1.3 fusion.36
  310.7 1.2 fusion.43
  321.1 1.8 broadcast_in_dim.66
  322.9 2.1 reshape.630
  325.6 4.8 %collective-permute-start.4 = (bf16[4,1,64,192]{3,2,1,0:T(8,128)(2,1)}, bf16[4,1,64,192]{3,2,1,0:T(8,128)(2,1)S(1)}, u32[]{:S(2)}, u32[]{:S(2)}) collective-permute-start(bf16[4,1,64,192]{3,2,1,0:T(8,128)(2,1)} %get-tuple-element.125), channel_id=1, source_target_pairs={{0,1},{1,2},{2,3},{3,4},{4,5},{5,6},{6,7},{8,9},{9,10},{10,11},{11... | collective-permute-start | bytes 294920 | tf_op jit(solution)/shard_map/ppermute | solution.py:19
  330.5 1.9 collective-permute-start.5
  332.4 1.4 fusion.187
  333.8 2.8 reshape.654
  337.0 2.0 fusion.9
  339.0 3.1 fusion.185
  342.1 7.9 %fusion.184 = (bf16[4,8,64,192]{3,2,1,0:T(8,128)(2,1)S(1)}, bf16[4,8,64,192]{3,2,1,0:T(8,128)(2,1)S(1)}, bf16[4,8,64,192]{3,2,1,0:T(8,128)(2,1)S(1)}, bf16[4,8,6...) fusion(bf16[6,10,66,192]{3,2,1,0:T(8,128)(2,1)S(1)} %fusion.9), kind=kLoop, calls=%fused_computation.298 | loop fusion | bytes 29884416 | tf_op jit(solution)/shard_map/slice | solution.py:45
  372.6 1.0 select_convert_fusion
  (582 shorter events, 124.9 us)
Async XLA Ops:
  6.5 124.8 %copy-start.92 = (bf16[3,27,96]{2,1,0:T(8,128)(2,1)S(1)}, bf16[3,27,96]{2,1,0:T(8,128)(2,1)}, u32[]{:S(2)}) copy-start(bf16[3,27,96]{2,1,0:T(8,128)(2,1)} %param.16) | copy-start | bytes 46660
  95.1 27.9 %all-to-all-start = ((bf16[64,2,128]{2,1,0:T(2,128)(2,1)}), bf16[64,2,128]{2,1,0:T(2,128)(2,1)S(1)}, u32[]{:S(2)}, u32[]{:S(2)}) async-start(bf16[64,2,128]{2,1,0:T(2,128)(2,1)} %reshape.708), calls=%async_computation | async-start | bytes 65536 | tf_op jit(solution)/shard_map/all_to_all | solution.py:81
  112.2 128.1 %all-gather.2.cloned.1.call-start = ((), (), s32[]{:S(2)}) async-start(), calls=%async_computation.2 | async-start | bytes 6389760 | tf_op jit(solution)/shard_map/all_gather | solution.py:110
  124.2 15.3 %collective-permute-start = (bf16[4,1,16,16]{3,2,1,0:T(8,128)(2,1)S(1)}, bf16[4,1,16,16]{3,2,1,0:T(8,128)(2,1)S(1)}, u32[]{:S(2)}, u32[]{:S(2)}) collective-permute-start(bf16[4,1,16,16]{3,2,1,0:T(8,128)(2,1)S(1)} %get-tuple-element.157), channel_id=1, source_target_pairs={{0,1},{1,2},{2,3},{3,4},{4,5},{5,6},{6,7},{8,9},{9,10},{10,11},{11... | collective-permute-start | bytes 6152 | tf_op jit(solution)/shard_map/ppermute | solution.py:19
  129.3 10.2 %collective-permute-start.1 = (bf16[4,1,16,16]{3,2,1,0:T(8,128)(2,1)S(1)}, bf16[4,1,16,16]{3,2,1,0:T(8,128)(2,1)S(1)}, u32[]{:S(2)}, u32[]{:S(2)}) collective-permute-start(bf16[4,1,16,16]{3,2,1,0:T(8,128)(2,1)S(1)} %get-tuple-element.158), channel_id=1, source_target_pairs={{1,0},{2,1},{3,2},{4,3},{5,4},{6,5},{7,6},{9,8},{10,9},{11,10},{12... | collective-permute-start | bytes 6152 | tf_op jit(solution)/shard_map/ppermute | solution.py:21
  132.7 6.9 %copy-start.69 = (bf16[16,27,384]{2,0,1:T(8,128)(2,1)S(1)}, bf16[16,27,384]{2,0,1:T(8,128)(2,1)}, u32[]{:S(2)}) copy-start(bf16[16,27,384]{2,0,1:T(8,128)(2,1)} %param.14) | copy-start | bytes 995332
  132.7 48.5 %all-to-all-start.1 = ((bf16[64,3,27,96]{3,2,1,0:T(8,128)(2,1)}), bf16[64,3,27,96]{3,2,1,0:T(8,128)(2,1)S(1)}, u32[]{:S(2)}, u32[]{:S(2)}) async-start(bf16[64,3,27,96]{3,2,1,0:T(8,128)(2,1)} %stack.2), calls=%async_computation.1 | async-start | bytes 3145728 | tf_op jit(solution)/shard_map/all_to_all | solution.py:99
  142.5 1.6 copy-start.93
  143.2 7.7 %copy-start.95 = (f32[96]{0:T(128)S(1)}, f32[96]{0:T(128)}, u32[]{:S(2)}) copy-start(f32[96]{0:T(128)} %param.19) | copy-start | bytes 1156
  144.6 7.9 %collective-permute-start.2 = (bf16[4,1,32,384]{3,2,1,0:T(8,128)(2,1)S(1)}, bf16[4,1,32,384]{3,2,1,0:T(8,128)(2,1)S(1)}, u32[]{:S(2)}, u32[]{:S(2)}) collective-permute-start(bf16[4,1,32,384]{3,2,1,0:T(8,128)(2,1)S(1)} %get-tuple-element.129), channel_id=1, source_target_pairs={{0,1},{1,2},{2,3},{3,4},{4,5},{5,6},{6,7},{8,9},{9,10},{10,11},{11... | collective-permute-start | bytes 294920 | tf_op jit(solution)/shard_map/ppermute | solution.py:19
  148.6 6.3 %collective-permute-start.3 = (bf16[4,1,32,384]{3,2,1,0:T(8,128)(2,1)S(1)}, bf16[4,1,32,384]{3,2,1,0:T(8,128)(2,1)S(1)}, u32[]{:S(2)}, u32[]{:S(2)}) collective-permute-start(bf16[4,1,32,384]{3,2,1,0:T(8,128)(2,1)S(1)} %get-tuple-element.130), channel_id=1, source_target_pairs={{1,0},{2,1},{3,2},{4,3},{5,4},{6,5},{7,6},{9,8},{10,9},{11,10},{12... | collective-permute-start | bytes 294920 | tf_op jit(solution)/shard_map/ppermute | solution.py:21
  296.0 12.1 %copy-start.22 = (bf16[4,4,32,384]{3,2,1,0:T(8,128)(2,1)S(1)}, bf16[4,4,32,384]{3,2,1,0:T(8,128)(2,1)}, u32[]{:S(2)}) copy-start(bf16[4,4,32,384]{3,2,1,0:T(8,128)(2,1)} %get-tuple-element.121) | copy-start | bytes 1179652
  299.0 10.4 %copy-start.21 = (bf16[4,4,32,384]{3,2,1,0:T(8,128)(2,1)S(1)}, bf16[4,4,32,384]{3,2,1,0:T(8,128)(2,1)}, u32[]{:S(2)}) copy-start(bf16[4,4,32,384]{3,2,1,0:T(8,128)(2,1)} %get-tuple-element.122) | copy-start | bytes 1179652
  300.2 10.5 %copy-start.23 = (bf16[4,4,32,384]{3,2,1,0:T(8,128)(2,1)S(1)}, bf16[4,4,32,384]{3,2,1,0:T(8,128)(2,1)}, u32[]{:S(2)}) copy-start(bf16[4,4,32,384]{3,2,1,0:T(8,128)(2,1)} %get-tuple-element.102) | copy-start | bytes 1179652
  306.8 5.5 %copy-start.43 = (bf16[4,4,32,384]{3,2,1,0:T(8,128)(2,1)S(1)}, bf16[4,4,32,384]{3,2,1,0:T(8,128)(2,1)}, u32[]{:S(2)}) copy-start(bf16[4,4,32,384]{3,2,1,0:T(8,128)(2,1)} %get-tuple-element.119) | copy-start | bytes 1179652
  308.1 3.8 %copy-start.44 = (bf16[4,4,32,384]{3,2,1,0:T(8,128)(2,1)S(1)}, bf16[4,4,32,384]{3,2,1,0:T(8,128)(2,1)}, u32[]{:S(2)}) copy-start(bf16[4,4,32,384]{3,2,1,0:T(8,128)(2,1)} %get-tuple-element.120) | copy-start | bytes 1179652
  308.1 3.8 %copy-start.61 = (bf16[384,1,192]{0,2,1:T(8,128)(2,1)S(1)}, bf16[384,1,192]{0,2,1:T(8,128)(2,1)}, u32[]{:S(2)}) copy-start(bf16[384,1,192]{0,2,1:T(8,128)(2,1)} %copy.106) | copy-start | bytes 442372
  308.1 4.2 %copy-start.59 = (bf16[384,1,192]{0,2,1:T(8,128)(2,1)S(1)}, bf16[384,1,192]{0,2,1:T(8,128)(2,1)}, u32[]{:S(2)}) copy-start(bf16[384,1,192]{0,2,1:T(8,128)(2,1)} %copy.107) | copy-start | bytes 442372
  309.4 3.2 copy-start.42
  309.4 3.2 copy-start.57
  312.6 1.1 copy-start.51
  313.0 1.1 copy-start.68
  313.3 1.1 copy-start.67
  313.7 1.1 copy-start.36
  313.7 1.1 copy-start.66
  314.0 1.1 copy-start.65
  314.4 1.1 copy-start.64
  314.7 1.1 copy-start.63
  315.1 1.1 copy-start.62
  315.5 1.1 copy-start.60
  315.8 1.1 copy-start.58
  316.2 1.1 copy-start.56
  316.5 1.1 copy-start.54
  316.9 1.1 copy-start.52
  317.2 1.1 copy-start.50
  317.6 1.1 copy-start.49
  317.9 1.1 copy-start.48
  318.3 1.1 copy-start.47
  318.7 1.1 copy-start.46
  319.1 1.1 copy-start.45
  325.6 11.0 %collective-permute-start.4 = (bf16[4,1,64,192]{3,2,1,0:T(8,128)(2,1)}, bf16[4,1,64,192]{3,2,1,0:T(8,128)(2,1)S(1)}, u32[]{:S(2)}, u32[]{:S(2)}) collective-permute-start(bf16[4,1,64,192]{3,2,1,0:T(8,128)(2,1)} %get-tuple-element.125), channel_id=1, source_target_pairs={{0,1},{1,2},{2,3},{3,4},{4,5},{5,6},{6,7},{8,9},{9,10},{10,11},{11... | collective-permute-start | bytes 294920 | tf_op jit(solution)/shard_map/ppermute | solution.py:19
  330.5 6.5 %collective-permute-start.5 = (bf16[4,1,64,192]{3,2,1,0:T(8,128)(2,1)}, bf16[4,1,64,192]{3,2,1,0:T(8,128)(2,1)S(1)}, u32[]{:S(2)}, u32[]{:S(2)}) collective-permute-start(bf16[4,1,64,192]{3,2,1,0:T(8,128)(2,1)} %get-tuple-element.126), channel_id=1, source_target_pairs={{1,0},{2,1},{3,2},{4,3},{5,4},{6,5},{7,6},{9,8},{10,9},{11,10},{12... | collective-permute-start | bytes 294920 | tf_op jit(solution)/shard_map/ppermute | solution.py:21
  342.1 8.4 %copy-start.73 = (bf16[192,1,96]{2,1,0:T(2,128)(2,1)S(1)}, bf16[192,1,96]{2,1,0:T(2,128)(2,1)}, u32[]{:S(2)}) copy-start(bf16[192,1,96]{2,1,0:T(2,128)(2,1)} %get-tuple-element.73) | copy-start | bytes 110596
  350.5 1.2 copy-start.16
  350.5 1.2 copy-start.75
  351.0 1.3 copy-start.15
  351.0 1.3 copy-start.74
  351.7 1.3 copy-start.14
  352.3 1.3 copy-start.13
  353.0 1.3 copy-start.12
  353.6 1.3 copy-start.11
  354.3 1.3 copy-start.10
  354.9 1.3 copy-start.9
  355.7 1.4 copy-start.8
  356.6 1.4 copy-start.7
  357.6 1.4 copy-start.6
  358.6 1.4 copy-start.5
  359.5 1.4 copy-start.4
  360.5 1.4 copy-start.3
  361.5 1.4 copy-start.2
  367.5 1.2 copy-start.17
  367.5 1.2 copy-start.78
  367.9 1.2 copy-start.77
  371.7 2.0 copy-start.1
  (41 other events, 41.9 us)
Sparse Core Ops, SparseCore 0:
  131.4 108.8 all-gather.1
